TPU v7x, 256 devices: a whole 4x4x8 slice. The times are simulated.
256 devices in a mesh: freq: 4 (over y), mx: 8 (over x, core), my: 8 (over z).
Axes of the slice: x: 4, y: 4, z: 8, core: 2. Of those that a mesh axis runs over, the one named last changes fastest.
Arguments:
- adjoint_rhs: float32 [4, 2, 3, 512, 2048], P('freq', None, None, 'mx', 'my'), may hold values from -4 to 6
- state: bfloat16 [4, 2, 3, 512, 2048], P('freq', None, None, 'mx', 'my'), may hold values from -1.5 to 1.5
- density: float32 [512, 2048], P('mx', 'my'), may hold values from 0.85 to 1
- stiffness: float32 [512, 2048], P('mx', 'my'), may hold values from 1.5 to 4
- mass: float32 [512, 2048], P('mx', 'my'), may hold values from 0.2 to 1
- omega: float32 [4], P('freq'), may hold values from 0.15 to 0.45
- send_rows: int32 [64, 2048], P(('mx', 'my')), may hold values from 0 to 16383, as said below
- recv_rows: int32 [64, 2048], P(('mx', 'my')), may hold values from 0 to 16383, as said below
- mortar_weight: float32 [64, 2048], P(('mx', 'my')), may hold values from 0 to 1.5, as said below
Outputs:
- adjoint: float32 [4, 2, 3, 512, 2048], P('freq', None, None, 'mx', 'my')
- filtered_sensitivity: float32 [512, 2048], P('mx', 'my')
Inputs may be any that keep to these rules, and one draw needn't show every extreme that they name: `send_rows`: a local cell of the sending device; slots past the live count of a device pair hold 0. `recv_rows`: a local cell of the receiving device; empty slots hold 0. Live slots of a pair come first, up to 32 of them. `mortar_weight`: zero exactly in empty slots, at least 0.5 in live ones; every receiving device has a source device with all 32 slots live.
All inputs are finite; a program needn't handle non-finite values.
Results may differ from a plain program's by a relative error of at most 0.0003.
Values may be sent and summed in bfloat16 or wider, within the bound.
A program may use at most 64 MiB of HBM per device.

v0:
```python
import jax
import jax.numpy as jnp
from jax import lax
from jax.sharding import PartitionSpec as P

ITERS = 20


def extended(x, sides, width):
    for axis, dim in sides:
        size, length = (lax.axis_size(axis), x.shape[dim])
        up = [(i, (i + 1) % size) for i in range(size - 1)]
        down = [(j, i) for i, j in up]
        last = lax.slice_in_dim(x, length - width, length, axis=dim)
        first = lax.slice_in_dim(x, 0, width, axis=dim)
        before = lax.ppermute(last, axis, up)
        after = lax.ppermute(first, axis, down)
        x = jnp.concatenate([before, x, after], axis=dim)
    return x


def on_device(
    adjoint_rhs, state, density, stiffness, mass, omega, send_rows, recv_rows, mortar_weight
):
    rows_x, rows_y = density.shape
    cells = rows_x * rows_y
    w = omega[0]
    stiff = density**3 * stiffness
    dstiff = 3.0 * density**2 * stiffness
    rmass = density * mass
    sources = send_rows[0]
    targets = recv_rows[0]
    weights = mortar_weight[0]
    mdiag = jnp.zeros((cells,), jnp.float32).at[targets].add(weights).reshape(rows_x, rows_y)
    real_d = 4.4 * stiff + 0.3 + mdiag - w * w * rmass
    imag_d = 0.2 * w * (stiff + rmass)
    den = real_d * real_d + imag_d * imag_d
    rhs = adjoint_rhs.reshape(6, rows_x, rows_y)

    def mortar(field):
        sent = field.reshape(6, cells)[:, sources]
        got = lax.all_to_all(sent, ("mx", "my"), split_axis=1, concat_axis=1, tiled=True)
        added = jnp.zeros((6, cells), jnp.float32).at[:, targets].add(got * weights)
        return added.reshape(6, rows_x, rows_y)

    def sweep(step, field):
        padded = extended(field, (("mx", 1), ("my", 2)), 1)
        beside = (
            padded[:, 2:, 1:-1] + padded[:, :-2, 1:-1] + padded[:, 1:-1, 2:] + padded[:, 1:-1, :-2]
        )
        h = rhs + stiff * beside + mortar(field)
        new_re = (h[:3] * real_d + h[3:] * imag_d) / den
        new_im = (h[3:] * real_d - h[:3] * imag_d) / den
        return jnp.concatenate([new_re, new_im], axis=0)

    field = lax.fori_loop(0, ITERS, sweep, jnp.zeros((6, rows_x, rows_y), jnp.float32))
    state_six = state.reshape(6, rows_x, rows_y)
    state_pad = extended(state_six, (("mx", 1), ("my", 2)), 1).astype(jnp.float32)
    u = state_six.astype(jnp.float32)
    nb = (
        state_pad[:, 2:, 1:-1]
        + state_pad[:, :-2, 1:-1]
        + state_pad[:, 1:-1, 2:]
        + state_pad[:, 1:-1, :-2]
    )
    da = 4.4 * dstiff - w * w * mass
    db = 0.2 * w * (dstiff + mass)
    t_re = da * u[:3] - db * u[3:] - dstiff * nb[:3]
    t_im = da * u[3:] + db * u[:3] - dstiff * nb[3:]
    sens = -jnp.sum(field[:3] * t_re - field[3:] * t_im, axis=0)
    total = lax.psum(sens, "freq")
    weighted = extended(density * total, (("mx", 0), ("my", 1)), 1)
    filt = weighted[1:-1, 1:-1]
    filt = filt + 0.5 * (
        weighted[2:, 1:-1] + weighted[:-2, 1:-1] + weighted[1:-1, 2:] + weighted[1:-1, :-2]
    )
    filt = filt + 0.25 * (
        weighted[2:, 2:] + weighted[:-2, :-2] + weighted[2:, :-2] + weighted[:-2, 2:]
    )
    return (field.reshape(1, 2, 3, rows_x, rows_y), filt / (4.0 * density))


def solution(mesh):
    return jax.shard_map(
        on_device,
        mesh=mesh,
        in_specs=(
            P("freq", None, None, "mx", "my"),
            P("freq", None, None, "mx", "my"),
            P("mx", "my"),
            P("mx", "my"),
            P("mx", "my"),
            P("freq"),
            P(("mx", "my"), None),
            P(("mx", "my"), None),
            P(("mx", "my"), None),
        ),
        out_specs=(P("freq", None, None, "mx", "my"), P("mx", "my")),
        check_vma=False,
    )
```

profile of v0, /device:TPU:98, one launch (start us, length us, event | category | flops | bytes accessed | tf_op | source)
XLA Modules:
  0.0 1374.9 jit_solution(1580240488645792618)
XLA Ops:
  13.7 11.6 scatter_custom_fusion.1
  41.8 1255.3 %while.10 = (s32[]{:T(128)}, f32[6,64,256]{2,1,0:T(8,128)S(1)}, f32[64,256]{1,0:T(8,128)S(1)}, f32[6,64,256]{2,1,0:T(8,128)}, s32[2048]{0:T(1024)}, /*index=5*/s...) while((s32[]{:T(128)}, f32[6,64,256]{2,1,0:T(8,128)S(1)}, ...), condition=%wide.region_3.0_spmd, body=%wide.region_1.0_spmd.sunk | while | flops 2109442 | bytes 9095261 | solution.py:56
  46.6 8.8 gather_fusion
  56.7 11.4 all-to-all-start
  83.9 15.2 %scatter_custom_fusion.7 = f32[6,16384]{0,1:T(8,128)} fusion(s32[2048]{0:T(1024)S(1)} %bitcast.65, f32[2048,6]{1,0:T(8,128)S(1)} %copy.34, f32[]{:T(128)} %constant.21.clone.1..sunk), kind=kCustom, calls=%fused_computation.3.clone.1 | custom fusion | flops 12288 | bytes 393220 | tf_op jit(solution)/shard_map/while/body/eval_jaxpr/scatter-add | solution.py:43
  109.8 8.8 gather_fusion
  119.9 10.9 all-to-all-start
  146.7 15.2 %scatter_custom_fusion.7 = f32[6,16384]{0,1:T(8,128)} fusion(s32[2048]{0:T(1024)S(1)} %bitcast.65, f32[2048,6]{1,0:T(8,128)S(1)} %copy.34, f32[]{:T(128)} %constant.21.clone.1..sunk), kind=kCustom, calls=%fused_computation.3.clone.1 | custom fusion | flops 12288 | bytes 393220 | tf_op jit(solution)/shard_map/while/body/eval_jaxpr/scatter-add | solution.py:43
  172.5 8.8 gather_fusion
  182.6 10.9 all-to-all-start
  209.4 15.2 %scatter_custom_fusion.7 = f32[6,16384]{0,1:T(8,128)} fusion(s32[2048]{0:T(1024)S(1)} %bitcast.65, f32[2048,6]{1,0:T(8,128)S(1)} %copy.34, f32[]{:T(128)} %constant.21.clone.1..sunk), kind=kCustom, calls=%fused_computation.3.clone.1 | custom fusion | flops 12288 | bytes 393220 | tf_op jit(solution)/shard_map/while/body/eval_jaxpr/scatter-add | solution.py:43
  235.3 8.8 gather_fusion
  245.4 10.9 all-to-all-start
  272.1 15.2 %scatter_custom_fusion.7 = f32[6,16384]{0,1:T(8,128)} fusion(s32[2048]{0:T(1024)S(1)} %bitcast.65, f32[2048,6]{1,0:T(8,128)S(1)} %copy.34, f32[]{:T(128)} %constant.21.clone.1..sunk), kind=kCustom, calls=%fused_computation.3.clone.1 | custom fusion | flops 12288 | bytes 393220 | tf_op jit(solution)/shard_map/while/body/eval_jaxpr/scatter-add | solution.py:43
  298.0 8.8 gather_fusion
  308.1 10.9 all-to-all-start
  334.9 15.2 %scatter_custom_fusion.7 = f32[6,16384]{0,1:T(8,128)} fusion(s32[2048]{0:T(1024)S(1)} %bitcast.65, f32[2048,6]{1,0:T(8,128)S(1)} %copy.34, f32[]{:T(128)} %constant.21.clone.1..sunk), kind=kCustom, calls=%fused_computation.3.clone.1 | custom fusion | flops 12288 | bytes 393220 | tf_op jit(solution)/shard_map/while/body/eval_jaxpr/scatter-add | solution.py:43
  370.8 10.9 all-to-all-start
  397.6 15.2 %scatter_custom_fusion.7 = f32[6,16384]{0,1:T(8,128)} fusion(s32[2048]{0:T(1024)S(1)} %bitcast.65, f32[2048,6]{1,0:T(8,128)S(1)} %copy.34, f32[]{:T(128)} %constant.21.clone.1..sunk), kind=kCustom, calls=%fused_computation.3.clone.1 | custom fusion | flops 12288 | bytes 393220 | tf_op jit(solution)/shard_map/while/body/eval_jaxpr/scatter-add | solution.py:43
  433.6 10.9 all-to-all-start
  460.4 15.2 %scatter_custom_fusion.7 = f32[6,16384]{0,1:T(8,128)} fusion(s32[2048]{0:T(1024)S(1)} %bitcast.65, f32[2048,6]{1,0:T(8,128)S(1)} %copy.34, f32[]{:T(128)} %constant.21.clone.1..sunk), kind=kCustom, calls=%fused_computation.3.clone.1 | custom fusion | flops 12288 | bytes 393220 | tf_op jit(solution)/shard_map/while/body/eval_jaxpr/scatter-add | solution.py:43
  496.3 10.9 all-to-all-start
  523.1 15.2 %scatter_custom_fusion.7 = f32[6,16384]{0,1:T(8,128)} fusion(s32[2048]{0:T(1024)S(1)} %bitcast.65, f32[2048,6]{1,0:T(8,128)S(1)} %copy.34, f32[]{:T(128)} %constant.21.clone.1..sunk), kind=kCustom, calls=%fused_computation.3.clone.1 | custom fusion | flops 12288 | bytes 393220 | tf_op jit(solution)/shard_map/while/body/eval_jaxpr/scatter-add | solution.py:43
  559.1 10.9 all-to-all-start
  585.8 15.2 %scatter_custom_fusion.7 = f32[6,16384]{0,1:T(8,128)} fusion(s32[2048]{0:T(1024)S(1)} %bitcast.65, f32[2048,6]{1,0:T(8,128)S(1)} %copy.34, f32[]{:T(128)} %constant.21.clone.1..sunk), kind=kCustom, calls=%fused_computation.3.clone.1 | custom fusion | flops 12288 | bytes 393220 | tf_op jit(solution)/shard_map/while/body/eval_jaxpr/scatter-add | solution.py:43
  621.8 10.9 all-to-all-start
  648.6 15.2 %scatter_custom_fusion.7 = f32[6,16384]{0,1:T(8,128)} fusion(s32[2048]{0:T(1024)S(1)} %bitcast.65, f32[2048,6]{1,0:T(8,128)S(1)} %copy.34, f32[]{:T(128)} %constant.21.clone.1..sunk), kind=kCustom, calls=%fused_computation.3.clone.1 | custom fusion | flops 12288 | bytes 393220 | tf_op jit(solution)/shard_map/while/body/eval_jaxpr/scatter-add | solution.py:43
  684.5 10.9 all-to-all-start
  711.3 15.2 %scatter_custom_fusion.7 = f32[6,16384]{0,1:T(8,128)} fusion(s32[2048]{0:T(1024)S(1)} %bitcast.65, f32[2048,6]{1,0:T(8,128)S(1)} %copy.34, f32[]{:T(128)} %constant.21.clone.1..sunk), kind=kCustom, calls=%fused_computation.3.clone.1 | custom fusion | flops 12288 | bytes 393220 | tf_op jit(solution)/shard_map/while/body/eval_jaxpr/scatter-add | solution.py:43
  747.3 10.9 all-to-all-start
  774.1 15.2 %scatter_custom_fusion.7 = f32[6,16384]{0,1:T(8,128)} fusion(s32[2048]{0:T(1024)S(1)} %bitcast.65, f32[2048,6]{1,0:T(8,128)S(1)} %copy.34, f32[]{:T(128)} %constant.21.clone.1..sunk), kind=kCustom, calls=%fused_computation.3.clone.1 | custom fusion | flops 12288 | bytes 393220 | tf_op jit(solution)/shard_map/while/body/eval_jaxpr/scatter-add | solution.py:43
  810.0 10.9 all-to-all-start
  836.8 15.2 %scatter_custom_fusion.7 = f32[6,16384]{0,1:T(8,128)} fusion(s32[2048]{0:T(1024)S(1)} %bitcast.65, f32[2048,6]{1,0:T(8,128)S(1)} %copy.34, f32[]{:T(128)} %constant.21.clone.1..sunk), kind=kCustom, calls=%fused_computation.3.clone.1 | custom fusion | flops 12288 | bytes 393220 | tf_op jit(solution)/shard_map/while/body/eval_jaxpr/scatter-add | solution.py:43
  872.8 10.9 all-to-all-start
  899.5 15.2 %scatter_custom_fusion.7 = f32[6,16384]{0,1:T(8,128)} fusion(s32[2048]{0:T(1024)S(1)} %bitcast.65, f32[2048,6]{1,0:T(8,128)S(1)} %copy.34, f32[]{:T(128)} %constant.21.clone.1..sunk), kind=kCustom, calls=%fused_computation.3.clone.1 | custom fusion | flops 12288 | bytes 393220 | tf_op jit(solution)/shard_map/while/body/eval_jaxpr/scatter-add | solution.py:43
  935.5 10.9 all-to-all-start
  962.3 15.2 %scatter_custom_fusion.7 = f32[6,16384]{0,1:T(8,128)} fusion(s32[2048]{0:T(1024)S(1)} %bitcast.65, f32[2048,6]{1,0:T(8,128)S(1)} %copy.34, f32[]{:T(128)} %constant.21.clone.1..sunk), kind=kCustom, calls=%fused_computation.3.clone.1 | custom fusion | flops 12288 | bytes 393220 | tf_op jit(solution)/shard_map/while/body/eval_jaxpr/scatter-add | solution.py:43
  998.2 10.9 all-to-all-start
  1025.0 15.2 %scatter_custom_fusion.7 = f32[6,16384]{0,1:T(8,128)} fusion(s32[2048]{0:T(1024)S(1)} %bitcast.65, f32[2048,6]{1,0:T(8,128)S(1)} %copy.34, f32[]{:T(128)} %constant.21.clone.1..sunk), kind=kCustom, calls=%fused_computation.3.clone.1 | custom fusion | flops 12288 | bytes 393220 | tf_op jit(solution)/shard_map/while/body/eval_jaxpr/scatter-add | solution.py:43
  1061.0 10.9 all-to-all-start
  1087.8 15.2 %scatter_custom_fusion.7 = f32[6,16384]{0,1:T(8,128)} fusion(s32[2048]{0:T(1024)S(1)} %bitcast.65, f32[2048,6]{1,0:T(8,128)S(1)} %copy.34, f32[]{:T(128)} %constant.21.clone.1..sunk), kind=kCustom, calls=%fused_computation.3.clone.1 | custom fusion | flops 12288 | bytes 393220 | tf_op jit(solution)/shard_map/while/body/eval_jaxpr/scatter-add | solution.py:43
  1123.7 10.9 all-to-all-start
  1150.5 15.2 %scatter_custom_fusion.7 = f32[6,16384]{0,1:T(8,128)} fusion(s32[2048]{0:T(1024)S(1)} %bitcast.65, f32[2048,6]{1,0:T(8,128)S(1)} %copy.34, f32[]{:T(128)} %constant.21.clone.1..sunk), kind=kCustom, calls=%fused_computation.3.clone.1 | custom fusion | flops 12288 | bytes 393220 | tf_op jit(solution)/shard_map/while/body/eval_jaxpr/scatter-add | solution.py:43
  1186.5 10.9 all-to-all-start
  1213.2 15.2 %scatter_custom_fusion.7 = f32[6,16384]{0,1:T(8,128)} fusion(s32[2048]{0:T(1024)S(1)} %bitcast.65, f32[2048,6]{1,0:T(8,128)S(1)} %copy.34, f32[]{:T(128)} %constant.21.clone.1..sunk), kind=kCustom, calls=%fused_computation.3.clone.1 | custom fusion | flops 12288 | bytes 393220 | tf_op jit(solution)/shard_map/while/body/eval_jaxpr/scatter-add | solution.py:43
  1249.2 10.9 all-to-all-start
  1276.0 15.2 %scatter_custom_fusion.7 = f32[6,16384]{0,1:T(8,128)} fusion(s32[2048]{0:T(1024)S(1)} %bitcast.65, f32[2048,6]{1,0:T(8,128)S(1)} %copy.34, f32[]{:T(128)} %constant.21.clone.1..sunk), kind=kCustom, calls=%fused_computation.3.clone.1 | custom fusion | flops 12288 | bytes 393220 | tf_op jit(solution)/shard_map/while/body/eval_jaxpr/scatter-add | solution.py:43
  1299.1 48.6 %all-reduce.2.cloned.1.call-done = f32[64,256]{1,0:T(8,128)} async-done(((f32[64,256]{1,0:T(8,128)}), f32[64,256]{1,0:T(8,128)}) %all-reduce.2.cloned.1.call-update) | async-done | bytes 65552 | tf_op jit(solution)/shard_map/psum | solution.py:71
  (798 shorter events, 727.4 us)
Async XLA Ops:
  7.2 1340.5 %all-reduce.2.cloned.1.call-start = ((), (), s32[]{:S(2)}) async-start(), calls=%async_computation.1 | async-start | bytes 131072 | tf_op jit(solution)/shard_map/psum | solution.py:71
  56.7 25.2 %all-to-all-start = ((f32[64,1,192]{2,1,0:T(1,128)}), f32[64,1,192]{2,1,0:T(1,128)S(1)}, u32[]{:S(2)}, u32[]{:S(2)}) async-start(f32[64,1,192]{2,1,0:T(1,128)} %reshape.136), calls=%async_computation | async-start | bytes 131072 | tf_op jit(solution)/shard_map/while/body/eval_jaxpr/all_to_all | solution.py:42
  75.4 29.1 %collective-permute-start.2 = (f32[6,66,1]{2,1,0:T(8,128)S(1)}, f32[6,66,1]{2,1,0:T(8,128)S(1)}, u32[]{:S(2)}, u32[]{:S(2)}) collective-permute-start(f32[6,66,1]{2,1,0:T(8,128)S(1)} %get-tuple-element.180), channel_id=1, source_target_pairs={{0,1},{1,2},{2,3},{3,4},{4,5},{5,6},{6,7},{8,9},{9,10},{10,11},{11... | collective-permute-start | bytes 4760 | tf_op jit(solution)/shard_map/while/body/eval_jaxpr/ppermute | solution.py:16
  80.0 24.5 %collective-permute-start.3 = (f32[6,66,1]{2,1,0:T(8,128)S(1)}, f32[6,66,1]{2,1,0:T(8,128)S(1)}, u32[]{:S(2)}, u32[]{:S(2)}) collective-permute-start(f32[6,66,1]{2,1,0:T(8,128)S(1)} %get-tuple-element.181), channel_id=1, source_target_pairs={{1,0},{2,1},{3,2},{4,3},{5,4},{6,5},{7,6},{9,8},{10,9},{11,10},{12... | collective-permute-start | bytes 4760 | tf_op jit(solution)/shard_map/while/body/eval_jaxpr/ppermute | solution.py:17
  119.9 24.8 %all-to-all-start = ((f32[64,1,192]{2,1,0:T(1,128)}), f32[64,1,192]{2,1,0:T(1,128)S(1)}, u32[]{:S(2)}, u32[]{:S(2)}) async-start(f32[64,1,192]{2,1,0:T(1,128)} %reshape.136), calls=%async_computation | async-start | bytes 131072 | tf_op jit(solution)/shard_map/while/body/eval_jaxpr/all_to_all | solution.py:42
  138.1 29.1 %collective-permute-start.2 = (f32[6,66,1]{2,1,0:T(8,128)S(1)}, f32[6,66,1]{2,1,0:T(8,128)S(1)}, u32[]{:S(2)}, u32[]{:S(2)}) collective-permute-start(f32[6,66,1]{2,1,0:T(8,128)S(1)} %get-tuple-element.180), channel_id=1, source_target_pairs={{0,1},{1,2},{2,3},{3,4},{4,5},{5,6},{6,7},{8,9},{9,10},{10,11},{11... | collective-permute-start | bytes 4760 | tf_op jit(solution)/shard_map/while/body/eval_jaxpr/ppermute | solution.py:16
  142.7 24.5 %collective-permute-start.3 = (f32[6,66,1]{2,1,0:T(8,128)S(1)}, f32[6,66,1]{2,1,0:T(8,128)S(1)}, u32[]{:S(2)}, u32[]{:S(2)}) collective-permute-start(f32[6,66,1]{2,1,0:T(8,128)S(1)} %get-tuple-element.181), channel_id=1, source_target_pairs={{1,0},{2,1},{3,2},{4,3},{5,4},{6,5},{7,6},{9,8},{10,9},{11,10},{12... | collective-permute-start | bytes 4760 | tf_op jit(solution)/shard_map/while/body/eval_jaxpr/ppermute | solution.py:17
  182.6 24.8 %all-to-all-start = ((f32[64,1,192]{2,1,0:T(1,128)}), f32[64,1,192]{2,1,0:T(1,128)S(1)}, u32[]{:S(2)}, u32[]{:S(2)}) async-start(f32[64,1,192]{2,1,0:T(1,128)} %reshape.136), calls=%async_computation | async-start | bytes 131072 | tf_op jit(solution)/shard_map/while/body/eval_jaxpr/all_to_all | solution.py:42
  200.9 29.1 %collective-permute-start.2 = (f32[6,66,1]{2,1,0:T(8,128)S(1)}, f32[6,66,1]{2,1,0:T(8,128)S(1)}, u32[]{:S(2)}, u32[]{:S(2)}) collective-permute-start(f32[6,66,1]{2,1,0:T(8,128)S(1)} %get-tuple-element.180), channel_id=1, source_target_pairs={{0,1},{1,2},{2,3},{3,4},{4,5},{5,6},{6,7},{8,9},{9,10},{10,11},{11... | collective-permute-start | bytes 4760 | tf_op jit(solution)/shard_map/while/body/eval_jaxpr/ppermute | solution.py:16
  205.5 24.5 %collective-permute-start.3 = (f32[6,66,1]{2,1,0:T(8,128)S(1)}, f32[6,66,1]{2,1,0:T(8,128)S(1)}, u32[]{:S(2)}, u32[]{:S(2)}) collective-permute-start(f32[6,66,1]{2,1,0:T(8,128)S(1)} %get-tuple-element.181), channel_id=1, source_target_pairs={{1,0},{2,1},{3,2},{4,3},{5,4},{6,5},{7,6},{9,8},{10,9},{11,10},{12... | collective-permute-start | bytes 4760 | tf_op jit(solution)/shard_map/while/body/eval_jaxpr/ppermute | solution.py:17
  245.4 24.8 %all-to-all-start = ((f32[64,1,192]{2,1,0:T(1,128)}), f32[64,1,192]{2,1,0:T(1,128)S(1)}, u32[]{:S(2)}, u32[]{:S(2)}) async-start(f32[64,1,192]{2,1,0:T(1,128)} %reshape.136), calls=%async_computation | async-start | bytes 131072 | tf_op jit(solution)/shard_map/while/body/eval_jaxpr/all_to_all | solution.py:42
  263.6 29.1 %collective-permute-start.2 = (f32[6,66,1]{2,1,0:T(8,128)S(1)}, f32[6,66,1]{2,1,0:T(8,128)S(1)}, u32[]{:S(2)}, u32[]{:S(2)}) collective-permute-start(f32[6,66,1]{2,1,0:T(8,128)S(1)} %get-tuple-element.180), channel_id=1, source_target_pairs={{0,1},{1,2},{2,3},{3,4},{4,5},{5,6},{6,7},{8,9},{9,10},{10,11},{11... | collective-permute-start | bytes 4760 | tf_op jit(solution)/shard_map/while/body/eval_jaxpr/ppermute | solution.py:16
  268.2 24.5 %collective-permute-start.3 = (f32[6,66,1]{2,1,0:T(8,128)S(1)}, f32[6,66,1]{2,1,0:T(8,128)S(1)}, u32[]{:S(2)}, u32[]{:S(2)}) collective-permute-start(f32[6,66,1]{2,1,0:T(8,128)S(1)} %get-tuple-element.181), channel_id=1, source_target_pairs={{1,0},{2,1},{3,2},{4,3},{5,4},{6,5},{7,6},{9,8},{10,9},{11,10},{12... | collective-permute-start | bytes 4760 | tf_op jit(solution)/shard_map/while/body/eval_jaxpr/ppermute | solution.py:17
  308.1 24.8 %all-to-all-start = ((f32[64,1,192]{2,1,0:T(1,128)}), f32[64,1,192]{2,1,0:T(1,128)S(1)}, u32[]{:S(2)}, u32[]{:S(2)}) async-start(f32[64,1,192]{2,1,0:T(1,128)} %reshape.136), calls=%async_computation | async-start | bytes 131072 | tf_op jit(solution)/shard_map/while/body/eval_jaxpr/all_to_all | solution.py:42
  326.4 29.1 %collective-permute-start.2 = (f32[6,66,1]{2,1,0:T(8,128)S(1)}, f32[6,66,1]{2,1,0:T(8,128)S(1)}, u32[]{:S(2)}, u32[]{:S(2)}) collective-permute-start(f32[6,66,1]{2,1,0:T(8,128)S(1)} %get-tuple-element.180), channel_id=1, source_target_pairs={{0,1},{1,2},{2,3},{3,4},{4,5},{5,6},{6,7},{8,9},{9,10},{10,11},{11... | collective-permute-start | bytes 4760 | tf_op jit(solution)/shard_map/while/body/eval_jaxpr/ppermute | solution.py:16
  330.9 24.5 %collective-permute-start.3 = (f32[6,66,1]{2,1,0:T(8,128)S(1)}, f32[6,66,1]{2,1,0:T(8,128)S(1)}, u32[]{:S(2)}, u32[]{:S(2)}) collective-permute-start(f32[6,66,1]{2,1,0:T(8,128)S(1)} %get-tuple-element.181), channel_id=1, source_target_pairs={{1,0},{2,1},{3,2},{4,3},{5,4},{6,5},{7,6},{9,8},{10,9},{11,10},{12... | collective-permute-start | bytes 4760 | tf_op jit(solution)/shard_map/while/body/eval_jaxpr/ppermute | solution.py:17
  370.8 24.8 %all-to-all-start = ((f32[64,1,192]{2,1,0:T(1,128)}), f32[64,1,192]{2,1,0:T(1,128)S(1)}, u32[]{:S(2)}, u32[]{:S(2)}) async-start(f32[64,1,192]{2,1,0:T(1,128)} %reshape.136), calls=%async_computation | async-start | bytes 131072 | tf_op jit(solution)/shard_map/while/body/eval_jaxpr/all_to_all | solution.py:42
  389.1 29.1 %collective-permute-start.2 = (f32[6,66,1]{2,1,0:T(8,128)S(1)}, f32[6,66,1]{2,1,0:T(8,128)S(1)}, u32[]{:S(2)}, u32[]{:S(2)}) collective-permute-start(f32[6,66,1]{2,1,0:T(8,128)S(1)} %get-tuple-element.180), channel_id=1, source_target_pairs={{0,1},{1,2},{2,3},{3,4},{4,5},{5,6},{6,7},{8,9},{9,10},{10,11},{11... | collective-permute-start | bytes 4760 | tf_op jit(solution)/shard_map/while/body/eval_jaxpr/ppermute | solution.py:16
  393.7 24.5 %collective-permute-start.3 = (f32[6,66,1]{2,1,0:T(8,128)S(1)}, f32[6,66,1]{2,1,0:T(8,128)S(1)}, u32[]{:S(2)}, u32[]{:S(2)}) collective-permute-start(f32[6,66,1]{2,1,0:T(8,128)S(1)} %get-tuple-element.181), channel_id=1, source_target_pairs={{1,0},{2,1},{3,2},{4,3},{5,4},{6,5},{7,6},{9,8},{10,9},{11,10},{12... | collective-permute-start | bytes 4760 | tf_op jit(solution)/shard_map/while/body/eval_jaxpr/ppermute | solution.py:17
  433.6 24.8 %all-to-all-start = ((f32[64,1,192]{2,1,0:T(1,128)}), f32[64,1,192]{2,1,0:T(1,128)S(1)}, u32[]{:S(2)}, u32[]{:S(2)}) async-start(f32[64,1,192]{2,1,0:T(1,128)} %reshape.136), calls=%async_computation | async-start | bytes 131072 | tf_op jit(solution)/shard_map/while/body/eval_jaxpr/all_to_all | solution.py:42
  451.8 29.1 %collective-permute-start.2 = (f32[6,66,1]{2,1,0:T(8,128)S(1)}, f32[6,66,1]{2,1,0:T(8,128)S(1)}, u32[]{:S(2)}, u32[]{:S(2)}) collective-permute-start(f32[6,66,1]{2,1,0:T(8,128)S(1)} %get-tuple-element.180), channel_id=1, source_target_pairs={{0,1},{1,2},{2,3},{3,4},{4,5},{5,6},{6,7},{8,9},{9,10},{10,11},{11... | collective-permute-start | bytes 4760 | tf_op jit(solution)/shard_map/while/body/eval_jaxpr/ppermute | solution.py:16
  456.4 24.5 %collective-permute-start.3 = (f32[6,66,1]{2,1,0:T(8,128)S(1)}, f32[6,66,1]{2,1,0:T(8,128)S(1)}, u32[]{:S(2)}, u32[]{:S(2)}) collective-permute-start(f32[6,66,1]{2,1,0:T(8,128)S(1)} %get-tuple-element.181), channel_id=1, source_target_pairs={{1,0},{2,1},{3,2},{4,3},{5,4},{6,5},{7,6},{9,8},{10,9},{11,10},{12... | collective-permute-start | bytes 4760 | tf_op jit(solution)/shard_map/while/body/eval_jaxpr/ppermute | solution.py:17
  496.3 24.8 %all-to-all-start = ((f32[64,1,192]{2,1,0:T(1,128)}), f32[64,1,192]{2,1,0:T(1,128)S(1)}, u32[]{:S(2)}, u32[]{:S(2)}) async-start(f32[64,1,192]{2,1,0:T(1,128)} %reshape.136), calls=%async_computation | async-start | bytes 131072 | tf_op jit(solution)/shard_map/while/body/eval_jaxpr/all_to_all | solution.py:42
  514.6 29.1 %collective-permute-start.2 = (f32[6,66,1]{2,1,0:T(8,128)S(1)}, f32[6,66,1]{2,1,0:T(8,128)S(1)}, u32[]{:S(2)}, u32[]{:S(2)}) collective-permute-start(f32[6,66,1]{2,1,0:T(8,128)S(1)} %get-tuple-element.180), channel_id=1, source_target_pairs={{0,1},{1,2},{2,3},{3,4},{4,5},{5,6},{6,7},{8,9},{9,10},{10,11},{11... | collective-permute-start | bytes 4760 | tf_op jit(solution)/shard_map/while/body/eval_jaxpr/ppermute | solution.py:16
  559.1 24.8 %all-to-all-start = ((f32[64,1,192]{2,1,0:T(1,128)}), f32[64,1,192]{2,1,0:T(1,128)S(1)}, u32[]{:S(2)}, u32[]{:S(2)}) async-start(f32[64,1,192]{2,1,0:T(1,128)} %reshape.136), calls=%async_computation | async-start | bytes 131072 | tf_op jit(solution)/shard_map/while/body/eval_jaxpr/all_to_all | solution.py:42
  577.3 29.1 %collective-permute-start.2 = (f32[6,66,1]{2,1,0:T(8,128)S(1)}, f32[6,66,1]{2,1,0:T(8,128)S(1)}, u32[]{:S(2)}, u32[]{:S(2)}) collective-permute-start(f32[6,66,1]{2,1,0:T(8,128)S(1)} %get-tuple-element.180), channel_id=1, source_target_pairs={{0,1},{1,2},{2,3},{3,4},{4,5},{5,6},{6,7},{8,9},{9,10},{10,11},{11... | collective-permute-start | bytes 4760 | tf_op jit(solution)/shard_map/while/body/eval_jaxpr/ppermute | solution.py:16
  621.8 24.8 %all-to-all-start = ((f32[64,1,192]{2,1,0:T(1,128)}), f32[64,1,192]{2,1,0:T(1,128)S(1)}, u32[]{:S(2)}, u32[]{:S(2)}) async-start(f32[64,1,192]{2,1,0:T(1,128)} %reshape.136), calls=%async_computation | async-start | bytes 131072 | tf_op jit(solution)/shard_map/while/body/eval_jaxpr/all_to_all | solution.py:42
  640.1 29.1 %collective-permute-start.2 = (f32[6,66,1]{2,1,0:T(8,128)S(1)}, f32[6,66,1]{2,1,0:T(8,128)S(1)}, u32[]{:S(2)}, u32[]{:S(2)}) collective-permute-start(f32[6,66,1]{2,1,0:T(8,128)S(1)} %get-tuple-element.180), channel_id=1, source_target_pairs={{0,1},{1,2},{2,3},{3,4},{4,5},{5,6},{6,7},{8,9},{9,10},{10,11},{11... | collective-permute-start | bytes 4760 | tf_op jit(solution)/shard_map/while/body/eval_jaxpr/ppermute | solution.py:16
  684.5 24.8 %all-to-all-start = ((f32[64,1,192]{2,1,0:T(1,128)}), f32[64,1,192]{2,1,0:T(1,128)S(1)}, u32[]{:S(2)}, u32[]{:S(2)}) async-start(f32[64,1,192]{2,1,0:T(1,128)} %reshape.136), calls=%async_computation | async-start | bytes 131072 | tf_op jit(solution)/shard_map/while/body/eval_jaxpr/all_to_all | solution.py:42
  702.8 29.1 %collective-permute-start.2 = (f32[6,66,1]{2,1,0:T(8,128)S(1)}, f32[6,66,1]{2,1,0:T(8,128)S(1)}, u32[]{:S(2)}, u32[]{:S(2)}) collective-permute-start(f32[6,66,1]{2,1,0:T(8,128)S(1)} %get-tuple-element.180), channel_id=1, source_target_pairs={{0,1},{1,2},{2,3},{3,4},{4,5},{5,6},{6,7},{8,9},{9,10},{10,11},{11... | collective-permute-start | bytes 4760 | tf_op jit(solution)/shard_map/while/body/eval_jaxpr/ppermute | solution.py:16
  747.3 24.8 %all-to-all-start = ((f32[64,1,192]{2,1,0:T(1,128)}), f32[64,1,192]{2,1,0:T(1,128)S(1)}, u32[]{:S(2)}, u32[]{:S(2)}) async-start(f32[64,1,192]{2,1,0:T(1,128)} %reshape.136), calls=%async_computation | async-start | bytes 131072 | tf_op jit(solution)/shard_map/while/body/eval_jaxpr/all_to_all | solution.py:42
  765.5 29.1 %collective-permute-start.2 = (f32[6,66,1]{2,1,0:T(8,128)S(1)}, f32[6,66,1]{2,1,0:T(8,128)S(1)}, u32[]{:S(2)}, u32[]{:S(2)}) collective-permute-start(f32[6,66,1]{2,1,0:T(8,128)S(1)} %get-tuple-element.180), channel_id=1, source_target_pairs={{0,1},{1,2},{2,3},{3,4},{4,5},{5,6},{6,7},{8,9},{9,10},{10,11},{11... | collective-permute-start | bytes 4760 | tf_op jit(solution)/shard_map/while/body/eval_jaxpr/ppermute | solution.py:16
  810.0 24.8 %all-to-all-start = ((f32[64,1,192]{2,1,0:T(1,128)}), f32[64,1,192]{2,1,0:T(1,128)S(1)}, u32[]{:S(2)}, u32[]{:S(2)}) async-start(f32[64,1,192]{2,1,0:T(1,128)} %reshape.136), calls=%async_computation | async-start | bytes 131072 | tf_op jit(solution)/shard_map/while/body/eval_jaxpr/all_to_all | solution.py:42
  828.3 29.1 %collective-permute-start.2 = (f32[6,66,1]{2,1,0:T(8,128)S(1)}, f32[6,66,1]{2,1,0:T(8,128)S(1)}, u32[]{:S(2)}, u32[]{:S(2)}) collective-permute-start(f32[6,66,1]{2,1,0:T(8,128)S(1)} %get-tuple-element.180), channel_id=1, source_target_pairs={{0,1},{1,2},{2,3},{3,4},{4,5},{5,6},{6,7},{8,9},{9,10},{10,11},{11... | collective-permute-start | bytes 4760 | tf_op jit(solution)/shard_map/while/body/eval_jaxpr/ppermute | solution.py:16
  872.8 24.8 %all-to-all-start = ((f32[64,1,192]{2,1,0:T(1,128)}), f32[64,1,192]{2,1,0:T(1,128)S(1)}, u32[]{:S(2)}, u32[]{:S(2)}) async-start(f32[64,1,192]{2,1,0:T(1,128)} %reshape.136), calls=%async_computation | async-start | bytes 131072 | tf_op jit(solution)/shard_map/while/body/eval_jaxpr/all_to_all | solution.py:42
  891.0 29.1 %collective-permute-start.2 = (f32[6,66,1]{2,1,0:T(8,128)S(1)}, f32[6,66,1]{2,1,0:T(8,128)S(1)}, u32[]{:S(2)}, u32[]{:S(2)}) collective-permute-start(f32[6,66,1]{2,1,0:T(8,128)S(1)} %get-tuple-element.180), channel_id=1, source_target_pairs={{0,1},{1,2},{2,3},{3,4},{4,5},{5,6},{6,7},{8,9},{9,10},{10,11},{11... | collective-permute-start | bytes 4760 | tf_op jit(solution)/shard_map/while/body/eval_jaxpr/ppermute | solution.py:16
  935.5 24.8 %all-to-all-start = ((f32[64,1,192]{2,1,0:T(1,128)}), f32[64,1,192]{2,1,0:T(1,128)S(1)}, u32[]{:S(2)}, u32[]{:S(2)}) async-start(f32[64,1,192]{2,1,0:T(1,128)} %reshape.136), calls=%async_computation | async-start | bytes 131072 | tf_op jit(solution)/shard_map/while/body/eval_jaxpr/all_to_all | solution.py:42
  953.8 29.1 %collective-permute-start.2 = (f32[6,66,1]{2,1,0:T(8,128)S(1)}, f32[6,66,1]{2,1,0:T(8,128)S(1)}, u32[]{:S(2)}, u32[]{:S(2)}) collective-permute-start(f32[6,66,1]{2,1,0:T(8,128)S(1)} %get-tuple-element.180), channel_id=1, source_target_pairs={{0,1},{1,2},{2,3},{3,4},{4,5},{5,6},{6,7},{8,9},{9,10},{10,11},{11... | collective-permute-start | bytes 4760 | tf_op jit(solution)/shard_map/while/body/eval_jaxpr/ppermute | solution.py:16
  998.2 24.8 %all-to-all-start = ((f32[64,1,192]{2,1,0:T(1,128)}), f32[64,1,192]{2,1,0:T(1,128)S(1)}, u32[]{:S(2)}, u32[]{:S(2)}) async-start(f32[64,1,192]{2,1,0:T(1,128)} %reshape.136), calls=%async_computation | async-start | bytes 131072 | tf_op jit(solution)/shard_map/while/body/eval_jaxpr/all_to_all | solution.py:42
  1016.5 29.1 %collective-permute-start.2 = (f32[6,66,1]{2,1,0:T(8,128)S(1)}, f32[6,66,1]{2,1,0:T(8,128)S(1)}, u32[]{:S(2)}, u32[]{:S(2)}) collective-permute-start(f32[6,66,1]{2,1,0:T(8,128)S(1)} %get-tuple-element.180), channel_id=1, source_target_pairs={{0,1},{1,2},{2,3},{3,4},{4,5},{5,6},{6,7},{8,9},{9,10},{10,11},{11... | collective-permute-start | bytes 4760 | tf_op jit(solution)/shard_map/while/body/eval_jaxpr/ppermute | solution.py:16
  1061.0 24.8 %all-to-all-start = ((f32[64,1,192]{2,1,0:T(1,128)}), f32[64,1,192]{2,1,0:T(1,128)S(1)}, u32[]{:S(2)}, u32[]{:S(2)}) async-start(f32[64,1,192]{2,1,0:T(1,128)} %reshape.136), calls=%async_computation | async-start | bytes 131072 | tf_op jit(solution)/shard_map/while/body/eval_jaxpr/all_to_all | solution.py:42
  1079.2 29.1 %collective-permute-start.2 = (f32[6,66,1]{2,1,0:T(8,128)S(1)}, f32[6,66,1]{2,1,0:T(8,128)S(1)}, u32[]{:S(2)}, u32[]{:S(2)}) collective-permute-start(f32[6,66,1]{2,1,0:T(8,128)S(1)} %get-tuple-element.180), channel_id=1, source_target_pairs={{0,1},{1,2},{2,3},{3,4},{4,5},{5,6},{6,7},{8,9},{9,10},{10,11},{11... | collective-permute-start | bytes 4760 | tf_op jit(solution)/shard_map/while/body/eval_jaxpr/ppermute | solution.py:16
  1123.7 24.8 %all-to-all-start = ((f32[64,1,192]{2,1,0:T(1,128)}), f32[64,1,192]{2,1,0:T(1,128)S(1)}, u32[]{:S(2)}, u32[]{:S(2)}) async-start(f32[64,1,192]{2,1,0:T(1,128)} %reshape.136), calls=%async_computation | async-start | bytes 131072 | tf_op jit(solution)/shard_map/while/body/eval_jaxpr/all_to_all | solution.py:42
  1142.0 29.1 %collective-permute-start.2 = (f32[6,66,1]{2,1,0:T(8,128)S(1)}, f32[6,66,1]{2,1,0:T(8,128)S(1)}, u32[]{:S(2)}, u32[]{:S(2)}) collective-permute-start(f32[6,66,1]{2,1,0:T(8,128)S(1)} %get-tuple-element.180), channel_id=1, source_target_pairs={{0,1},{1,2},{2,3},{3,4},{4,5},{5,6},{6,7},{8,9},{9,10},{10,11},{11... | collective-permute-start | bytes 4760 | tf_op jit(solution)/shard_map/while/body/eval_jaxpr/ppermute | solution.py:16
  1186.5 24.8 %all-to-all-start = ((f32[64,1,192]{2,1,0:T(1,128)}), f32[64,1,192]{2,1,0:T(1,128)S(1)}, u32[]{:S(2)}, u32[]{:S(2)}) async-start(f32[64,1,192]{2,1,0:T(1,128)} %reshape.136), calls=%async_computation | async-start | bytes 131072 | tf_op jit(solution)/shard_map/while/body/eval_jaxpr/all_to_all | solution.py:42
  1204.7 29.1 %collective-permute-start.2 = (f32[6,66,1]{2,1,0:T(8,128)S(1)}, f32[6,66,1]{2,1,0:T(8,128)S(1)}, u32[]{:S(2)}, u32[]{:S(2)}) collective-permute-start(f32[6,66,1]{2,1,0:T(8,128)S(1)} %get-tuple-element.180), channel_id=1, source_target_pairs={{0,1},{1,2},{2,3},{3,4},{4,5},{5,6},{6,7},{8,9},{9,10},{10,11},{11... | collective-permute-start | bytes 4760 | tf_op jit(solution)/shard_map/while/body/eval_jaxpr/ppermute | solution.py:16
  1249.2 24.8 %all-to-all-start = ((f32[64,1,192]{2,1,0:T(1,128)}), f32[64,1,192]{2,1,0:T(1,128)S(1)}, u32[]{:S(2)}, u32[]{:S(2)}) async-start(f32[64,1,192]{2,1,0:T(1,128)} %reshape.136), calls=%async_computation | async-start | bytes 131072 | tf_op jit(solution)/shard_map/while/body/eval_jaxpr/all_to_all | solution.py:42
  1267.5 29.1 %collective-permute-start.2 = (f32[6,66,1]{2,1,0:T(8,128)S(1)}, f32[6,66,1]{2,1,0:T(8,128)S(1)}, u32[]{:S(2)}, u32[]{:S(2)}) collective-permute-start(f32[6,66,1]{2,1,0:T(8,128)S(1)} %get-tuple-element.180), channel_id=1, source_target_pairs={{0,1},{1,2},{2,3},{3,4},{4,5},{5,6},{6,7},{8,9},{9,10},{10,11},{11... | collective-permute-start | bytes 4760 | tf_op jit(solution)/shard_map/while/body/eval_jaxpr/ppermute | solution.py:16
  (144 other events, 3909.9 us)
Sparse Core Ops, SparseCore 0:
  1299.2 48.4 all-reduce.1
where the time goes:
time: 1380 us; the launch traced here: 1370 us
  starting transfers between devices  458 us (33%)
  local copies, waits for them, and re-layouts  429 us (31%)
  other arithmetic  355 us (26%)
  waiting for transfers between devices  113 us (8%)
  between operations  14.9 us (1%)
    scatter-add x20, other arithmetic, mortar(): added = jnp.zeros((6, cells), jnp.float32).at[:, targets].add(got * weights)  304 us
    all_to_all x20, starting transfers between devices, mortar(): lax.all_to_all(sent, ('mx', 'my'), split_axis=1, concat_axis=1, tiled=True)  219 us
    gather x20, local copies, waits for them, and re-layouts, mortar(): sent = field.reshape(6, cells)[:, sources]  177 us
    ppermute x44, starting transfers between devices, extended(): before = lax.ppermute(last, axis, up)  149 us
    reshape x20, local copies, waits for them, and re-layouts, mortar(): return added.reshape(6, rows_x, rows_y)  106 us
    another operation x20, local copies, waits for them, and re-layouts  94.6 us
    ppermute x44, starting transfers between devices, extended(): after = lax.ppermute(first, axis, down)  89.9 us
    ppermute x44, waiting for transfers between devices, extended(): before = lax.ppermute(last, axis, up)  59.5 us
  transfers between devices with their start and end apart: 109, of which 25 were waited for; matrix products, arithmetic and copies ran while one was open for 34% of the time, Pallas kernels for 0%

commit v1 on v0

--- a/solution.py
+++ b/solution.py
@@ -68,7 +68,8 @@
     t_re = da * u[:3] - db * u[3:] - dstiff * nb[:3]
     t_im = da * u[3:] + db * u[:3] - dstiff * nb[3:]
     sens = -jnp.sum(field[:3] * t_re - field[3:] * t_im, axis=0)
-    total = lax.psum(sens, "freq")
+    parts = lax.all_gather(sens, "freq")
+    total = jnp.sum(parts, axis=0)
     weighted = extended(density * total, (("mx", 0), ("my", 1)), 1)
     filt = weighted[1:-1, 1:-1]
     filt = filt + 0.5 * (

time: 1380 us -> 1330 us (0.964)
  waiting for transfers between devices: 113 us -> 64.8 us
    psum x1 -> x0, waiting for transfers between devices: 48.6 us -> none  [on_device(): total = lax.psum(sens, 'freq')]
  transfers between devices with their start and end apart: 109 -> 108, of which waited for: 25 -> 24; matrix products, arithmetic and copies ran while one was open for 34% -> 35% of each run, Pallas kernels for 0% -> 0%
where the time goes in v1:
time: 1330 us; the launch traced here: 1320 us
  starting transfers between devices  458 us (34%)
  local copies, waits for them, and re-layouts  429 us (32%)
  other arithmetic  353 us (27%)
  waiting for transfers between devices  64.8 us (5%)
    scatter-add x20, other arithmetic, mortar(): added = jnp.zeros((6, cells), jnp.float32).at[:, targets].add(got * weights)  304 us
    all_to_all x20, starting transfers between devices, mortar(): lax.all_to_all(sent, ('mx', 'my'), split_axis=1, concat_axis=1, tiled=True)  219 us
    gather x20, local copies, waits for them, and re-layouts, mortar(): sent = field.reshape(6, cells)[:, sources]  177 us
    ppermute x44, starting transfers between devices, extended(): before = lax.ppermute(last, axis, up)  150 us
    reshape x20, local copies, waits for them, and re-layouts, mortar(): return added.reshape(6, rows_x, rows_y)  106 us
    another operation x20, local copies, waits for them, and re-layouts  94.2 us
    ppermute x44, starting transfers between devices, extended(): after = lax.ppermute(first, axis, down)  89.9 us
    ppermute x44, waiting for transfers between devices, extended(): before = lax.ppermute(last, axis, up)  59.5 us
  transfers between devices with their start and end apart: 108, of which 24 were waited for; matrix products, arithmetic and copies ran while one was open for 35% of the time, Pallas kernels for 0%

profile of v1, /device:TPU:98, one launch (start us, length us, event | category | flops | bytes accessed | tf_op | source)
XLA Modules:
  0.0 1324.3 jit_solution(2179315133609839198)
XLA Ops:
  7.1 11.6 scatter_custom_fusion.1
  35.2 1254.8 %while.10 = (s32[]{:T(128)}, f32[6,64,256]{2,1,0:T(8,128)S(1)}, f32[64,256]{1,0:T(8,128)S(1)}, f32[6,64,256]{2,1,0:T(8,128)}, s32[2048]{0:T(1024)}, /*index=5*/s...) while((s32[]{:T(128)}, f32[6,64,256]{2,1,0:T(8,128)S(1)}, ...), condition=%wide.region_3.0_spmd, body=%wide.region_1.0_spmd.sunk | while | flops 2109442 | bytes 9095261 | solution.py:56
  50.1 11.4 all-to-all-start
  77.3 15.2 %scatter_custom_fusion.7 = f32[6,16384]{0,1:T(8,128)} fusion(s32[2048]{0:T(1024)S(1)} %bitcast.67, f32[2048,6]{1,0:T(8,128)S(1)} %copy.39, f32[]{:T(128)} %constant.21.clone.1..sunk), kind=kCustom, calls=%fused_computation.3.clone.1 | custom fusion | flops 12288 | bytes 393220 | tf_op jit(solution)/shard_map/while/body/eval_jaxpr/scatter-add | solution.py:43
  113.2 10.9 all-to-all-start
  140.0 15.2 %scatter_custom_fusion.7 = f32[6,16384]{0,1:T(8,128)} fusion(s32[2048]{0:T(1024)S(1)} %bitcast.67, f32[2048,6]{1,0:T(8,128)S(1)} %copy.39, f32[]{:T(128)} %constant.21.clone.1..sunk), kind=kCustom, calls=%fused_computation.3.clone.1 | custom fusion | flops 12288 | bytes 393220 | tf_op jit(solution)/shard_map/while/body/eval_jaxpr/scatter-add | solution.py:43
  176.0 10.9 all-to-all-start
  202.8 15.2 %scatter_custom_fusion.7 = f32[6,16384]{0,1:T(8,128)} fusion(s32[2048]{0:T(1024)S(1)} %bitcast.67, f32[2048,6]{1,0:T(8,128)S(1)} %copy.39, f32[]{:T(128)} %constant.21.clone.1..sunk), kind=kCustom, calls=%fused_computation.3.clone.1 | custom fusion | flops 12288 | bytes 393220 | tf_op jit(solution)/shard_map/while/body/eval_jaxpr/scatter-add | solution.py:43
  228.6 8.8 gather_fusion
  238.7 10.9 all-to-all-start
  265.5 15.2 %scatter_custom_fusion.7 = f32[6,16384]{0,1:T(8,128)} fusion(s32[2048]{0:T(1024)S(1)} %bitcast.67, f32[2048,6]{1,0:T(8,128)S(1)} %copy.39, f32[]{:T(128)} %constant.21.clone.1..sunk), kind=kCustom, calls=%fused_computation.3.clone.1 | custom fusion | flops 12288 | bytes 393220 | tf_op jit(solution)/shard_map/while/body/eval_jaxpr/scatter-add | solution.py:43
  301.4 10.9 all-to-all-start
  328.2 15.2 %scatter_custom_fusion.7 = f32[6,16384]{0,1:T(8,128)} fusion(s32[2048]{0:T(1024)S(1)} %bitcast.67, f32[2048,6]{1,0:T(8,128)S(1)} %copy.39, f32[]{:T(128)} %constant.21.clone.1..sunk), kind=kCustom, calls=%fused_computation.3.clone.1 | custom fusion | flops 12288 | bytes 393220 | tf_op jit(solution)/shard_map/while/body/eval_jaxpr/scatter-add | solution.py:43
  364.1 10.9 all-to-all-start
  390.9 15.2 %scatter_custom_fusion.7 = f32[6,16384]{0,1:T(8,128)} fusion(s32[2048]{0:T(1024)S(1)} %bitcast.67, f32[2048,6]{1,0:T(8,128)S(1)} %copy.39, f32[]{:T(128)} %constant.21.clone.1..sunk), kind=kCustom, calls=%fused_computation.3.clone.1 | custom fusion | flops 12288 | bytes 393220 | tf_op jit(solution)/shard_map/while/body/eval_jaxpr/scatter-add | solution.py:43
  416.7 8.8 gather_fusion
  426.8 10.9 all-to-all-start
  453.6 15.2 %scatter_custom_fusion.7 = f32[6,16384]{0,1:T(8,128)} fusion(s32[2048]{0:T(1024)S(1)} %bitcast.67, f32[2048,6]{1,0:T(8,128)S(1)} %copy.39, f32[]{:T(128)} %constant.21.clone.1..sunk), kind=kCustom, calls=%fused_computation.3.clone.1 | custom fusion | flops 12288 | bytes 393220 | tf_op jit(solution)/shard_map/while/body/eval_jaxpr/scatter-add | solution.py:43
  489.6 10.9 all-to-all-start
  516.3 15.2 %scatter_custom_fusion.7 = f32[6,16384]{0,1:T(8,128)} fusion(s32[2048]{0:T(1024)S(1)} %bitcast.67, f32[2048,6]{1,0:T(8,128)S(1)} %copy.39, f32[]{:T(128)} %constant.21.clone.1..sunk), kind=kCustom, calls=%fused_computation.3.clone.1 | custom fusion | flops 12288 | bytes 393220 | tf_op jit(solution)/shard_map/while/body/eval_jaxpr/scatter-add | solution.py:43
  552.3 10.9 all-to-all-start
  579.1 15.2 %scatter_custom_fusion.7 = f32[6,16384]{0,1:T(8,128)} fusion(s32[2048]{0:T(1024)S(1)} %bitcast.67, f32[2048,6]{1,0:T(8,128)S(1)} %copy.39, f32[]{:T(128)} %constant.21.clone.1..sunk), kind=kCustom, calls=%fused_computation.3.clone.1 | custom fusion | flops 12288 | bytes 393220 | tf_op jit(solution)/shard_map/while/body/eval_jaxpr/scatter-add | solution.py:43
  604.9 8.8 gather_fusion
  615.0 10.9 all-to-all-start
  641.8 15.2 %scatter_custom_fusion.7 = f32[6,16384]{0,1:T(8,128)} fusion(s32[2048]{0:T(1024)S(1)} %bitcast.67, f32[2048,6]{1,0:T(8,128)S(1)} %copy.39, f32[]{:T(128)} %constant.21.clone.1..sunk), kind=kCustom, calls=%fused_computation.3.clone.1 | custom fusion | flops 12288 | bytes 393220 | tf_op jit(solution)/shard_map/while/body/eval_jaxpr/scatter-add | solution.py:43
  677.7 10.9 all-to-all-start
  704.5 15.2 %scatter_custom_fusion.7 = f32[6,16384]{0,1:T(8,128)} fusion(s32[2048]{0:T(1024)S(1)} %bitcast.67, f32[2048,6]{1,0:T(8,128)S(1)} %copy.39, f32[]{:T(128)} %constant.21.clone.1..sunk), kind=kCustom, calls=%fused_computation.3.clone.1 | custom fusion | flops 12288 | bytes 393220 | tf_op jit(solution)/shard_map/while/body/eval_jaxpr/scatter-add | solution.py:43
  730.3 8.8 gather_fusion
  740.4 10.9 all-to-all-start
  767.2 15.2 %scatter_custom_fusion.7 = f32[6,16384]{0,1:T(8,128)} fusion(s32[2048]{0:T(1024)S(1)} %bitcast.67, f32[2048,6]{1,0:T(8,128)S(1)} %copy.39, f32[]{:T(128)} %constant.21.clone.1..sunk), kind=kCustom, calls=%fused_computation.3.clone.1 | custom fusion | flops 12288 | bytes 393220 | tf_op jit(solution)/shard_map/while/body/eval_jaxpr/scatter-add | solution.py:43
  803.2 10.9 all-to-all-start
  829.9 15.2 %scatter_custom_fusion.7 = f32[6,16384]{0,1:T(8,128)} fusion(s32[2048]{0:T(1024)S(1)} %bitcast.67, f32[2048,6]{1,0:T(8,128)S(1)} %copy.39, f32[]{:T(128)} %constant.21.clone.1..sunk), kind=kCustom, calls=%fused_computation.3.clone.1 | custom fusion | flops 12288 | bytes 393220 | tf_op jit(solution)/shard_map/while/body/eval_jaxpr/scatter-add | solution.py:43
  865.9 10.9 all-to-all-start
  892.7 15.2 %scatter_custom_fusion.7 = f32[6,16384]{0,1:T(8,128)} fusion(s32[2048]{0:T(1024)S(1)} %bitcast.67, f32[2048,6]{1,0:T(8,128)S(1)} %copy.39, f32[]{:T(128)} %constant.21.clone.1..sunk), kind=kCustom, calls=%fused_computation.3.clone.1 | custom fusion | flops 12288 | bytes 393220 | tf_op jit(solution)/shard_map/while/body/eval_jaxpr/scatter-add | solution.py:43
  918.5 8.8 gather_fusion
  928.6 10.9 all-to-all-start
  955.4 15.2 %scatter_custom_fusion.7 = f32[6,16384]{0,1:T(8,128)} fusion(s32[2048]{0:T(1024)S(1)} %bitcast.67, f32[2048,6]{1,0:T(8,128)S(1)} %copy.39, f32[]{:T(128)} %constant.21.clone.1..sunk), kind=kCustom, calls=%fused_computation.3.clone.1 | custom fusion | flops 12288 | bytes 393220 | tf_op jit(solution)/shard_map/while/body/eval_jaxpr/scatter-add | solution.py:43
  991.3 10.9 all-to-all-start
  1018.1 15.2 %scatter_custom_fusion.7 = f32[6,16384]{0,1:T(8,128)} fusion(s32[2048]{0:T(1024)S(1)} %bitcast.67, f32[2048,6]{1,0:T(8,128)S(1)} %copy.39, f32[]{:T(128)} %constant.21.clone.1..sunk), kind=kCustom, calls=%fused_computation.3.clone.1 | custom fusion | flops 12288 | bytes 393220 | tf_op jit(solution)/shard_map/while/body/eval_jaxpr/scatter-add | solution.py:43
  1054.0 10.9 all-to-all-start
  1080.8 15.2 %scatter_custom_fusion.7 = f32[6,16384]{0,1:T(8,128)} fusion(s32[2048]{0:T(1024)S(1)} %bitcast.67, f32[2048,6]{1,0:T(8,128)S(1)} %copy.39, f32[]{:T(128)} %constant.21.clone.1..sunk), kind=kCustom, calls=%fused_computation.3.clone.1 | custom fusion | flops 12288 | bytes 393220 | tf_op jit(solution)/shard_map/while/body/eval_jaxpr/scatter-add | solution.py:43
  1116.8 10.9 all-to-all-start
  1143.5 15.2 %scatter_custom_fusion.7 = f32[6,16384]{0,1:T(8,128)} fusion(s32[2048]{0:T(1024)S(1)} %bitcast.67, f32[2048,6]{1,0:T(8,128)S(1)} %copy.39, f32[]{:T(128)} %constant.21.clone.1..sunk), kind=kCustom, calls=%fused_computation.3.clone.1 | custom fusion | flops 12288 | bytes 393220 | tf_op jit(solution)/shard_map/while/body/eval_jaxpr/scatter-add | solution.py:43
  1179.5 10.9 all-to-all-start
  1206.3 15.2 %scatter_custom_fusion.7 = f32[6,16384]{0,1:T(8,128)} fusion(s32[2048]{0:T(1024)S(1)} %bitcast.67, f32[2048,6]{1,0:T(8,128)S(1)} %copy.39, f32[]{:T(128)} %constant.21.clone.1..sunk), kind=kCustom, calls=%fused_computation.3.clone.1 | custom fusion | flops 12288 | bytes 393220 | tf_op jit(solution)/shard_map/while/body/eval_jaxpr/scatter-add | solution.py:43
  1242.2 10.9 all-to-all-start
  1269.0 15.2 %scatter_custom_fusion.7 = f32[6,16384]{0,1:T(8,128)} fusion(s32[2048]{0:T(1024)S(1)} %bitcast.67, f32[2048,6]{1,0:T(8,128)S(1)} %copy.39, f32[]{:T(128)} %constant.21.clone.1..sunk), kind=kCustom, calls=%fused_computation.3.clone.1 | custom fusion | flops 12288 | bytes 393220 | tf_op jit(solution)/shard_map/while/body/eval_jaxpr/scatter-add | solution.py:43
  1291.4 12.8 all-gather
  (797 shorter events, 726.1 us)
Async XLA Ops:
  50.1 25.2 %all-to-all-start = ((f32[64,1,192]{2,1,0:T(1,128)}), f32[64,1,192]{2,1,0:T(1,128)S(1)}, u32[]{:S(2)}, u32[]{:S(2)}) async-start(f32[64,1,192]{2,1,0:T(1,128)} %reshape.145), calls=%async_computation | async-start | bytes 131072 | tf_op jit(solution)/shard_map/while/body/eval_jaxpr/all_to_all | solution.py:42
  68.8 29.1 %collective-permute-start.2 = (f32[6,66,1]{2,1,0:T(8,128)S(1)}, f32[6,66,1]{2,1,0:T(8,128)S(1)}, u32[]{:S(2)}, u32[]{:S(2)}) collective-permute-start(f32[6,66,1]{2,1,0:T(8,128)S(1)} %get-tuple-element.180), channel_id=1, source_target_pairs={{0,1},{1,2},{2,3},{3,4},{4,5},{5,6},{6,7},{8,9},{9,10},{10,11},{11... | collective-permute-start | bytes 4760 | tf_op jit(solution)/shard_map/while/body/eval_jaxpr/ppermute | solution.py:16
  73.4 24.5 %collective-permute-start.3 = (f32[6,66,1]{2,1,0:T(8,128)S(1)}, f32[6,66,1]{2,1,0:T(8,128)S(1)}, u32[]{:S(2)}, u32[]{:S(2)}) collective-permute-start(f32[6,66,1]{2,1,0:T(8,128)S(1)} %get-tuple-element.181), channel_id=1, source_target_pairs={{1,0},{2,1},{3,2},{4,3},{5,4},{6,5},{7,6},{9,8},{10,9},{11,10},{12... | collective-permute-start | bytes 4760 | tf_op jit(solution)/shard_map/while/body/eval_jaxpr/ppermute | solution.py:17
  113.2 24.8 %all-to-all-start = ((f32[64,1,192]{2,1,0:T(1,128)}), f32[64,1,192]{2,1,0:T(1,128)S(1)}, u32[]{:S(2)}, u32[]{:S(2)}) async-start(f32[64,1,192]{2,1,0:T(1,128)} %reshape.145), calls=%async_computation | async-start | bytes 131072 | tf_op jit(solution)/shard_map/while/body/eval_jaxpr/all_to_all | solution.py:42
  131.5 29.1 %collective-permute-start.2 = (f32[6,66,1]{2,1,0:T(8,128)S(1)}, f32[6,66,1]{2,1,0:T(8,128)S(1)}, u32[]{:S(2)}, u32[]{:S(2)}) collective-permute-start(f32[6,66,1]{2,1,0:T(8,128)S(1)} %get-tuple-element.180), channel_id=1, source_target_pairs={{0,1},{1,2},{2,3},{3,4},{4,5},{5,6},{6,7},{8,9},{9,10},{10,11},{11... | collective-permute-start | bytes 4760 | tf_op jit(solution)/shard_map/while/body/eval_jaxpr/ppermute | solution.py:16
  176.0 24.8 %all-to-all-start = ((f32[64,1,192]{2,1,0:T(1,128)}), f32[64,1,192]{2,1,0:T(1,128)S(1)}, u32[]{:S(2)}, u32[]{:S(2)}) async-start(f32[64,1,192]{2,1,0:T(1,128)} %reshape.145), calls=%async_computation | async-start | bytes 131072 | tf_op jit(solution)/shard_map/while/body/eval_jaxpr/all_to_all | solution.py:42
  194.2 29.1 %collective-permute-start.2 = (f32[6,66,1]{2,1,0:T(8,128)S(1)}, f32[6,66,1]{2,1,0:T(8,128)S(1)}, u32[]{:S(2)}, u32[]{:S(2)}) collective-permute-start(f32[6,66,1]{2,1,0:T(8,128)S(1)} %get-tuple-element.180), channel_id=1, source_target_pairs={{0,1},{1,2},{2,3},{3,4},{4,5},{5,6},{6,7},{8,9},{9,10},{10,11},{11... | collective-permute-start | bytes 4760 | tf_op jit(solution)/shard_map/while/body/eval_jaxpr/ppermute | solution.py:16
  198.8 24.5 %collective-permute-start.3 = (f32[6,66,1]{2,1,0:T(8,128)S(1)}, f32[6,66,1]{2,1,0:T(8,128)S(1)}, u32[]{:S(2)}, u32[]{:S(2)}) collective-permute-start(f32[6,66,1]{2,1,0:T(8,128)S(1)} %get-tuple-element.181), channel_id=1, source_target_pairs={{1,0},{2,1},{3,2},{4,3},{5,4},{6,5},{7,6},{9,8},{10,9},{11,10},{12... | collective-permute-start | bytes 4760 | tf_op jit(solution)/shard_map/while/body/eval_jaxpr/ppermute | solution.py:17
  238.7 24.8 %all-to-all-start = ((f32[64,1,192]{2,1,0:T(1,128)}), f32[64,1,192]{2,1,0:T(1,128)S(1)}, u32[]{:S(2)}, u32[]{:S(2)}) async-start(f32[64,1,192]{2,1,0:T(1,128)} %reshape.145), calls=%async_computation | async-start | bytes 131072 | tf_op jit(solution)/shard_map/while/body/eval_jaxpr/all_to_all | solution.py:42
  256.9 29.1 %collective-permute-start.2 = (f32[6,66,1]{2,1,0:T(8,128)S(1)}, f32[6,66,1]{2,1,0:T(8,128)S(1)}, u32[]{:S(2)}, u32[]{:S(2)}) collective-permute-start(f32[6,66,1]{2,1,0:T(8,128)S(1)} %get-tuple-element.180), channel_id=1, source_target_pairs={{0,1},{1,2},{2,3},{3,4},{4,5},{5,6},{6,7},{8,9},{9,10},{10,11},{11... | collective-permute-start | bytes 4760 | tf_op jit(solution)/shard_map/while/body/eval_jaxpr/ppermute | solution.py:16
  301.4 24.8 %all-to-all-start = ((f32[64,1,192]{2,1,0:T(1,128)}), f32[64,1,192]{2,1,0:T(1,128)S(1)}, u32[]{:S(2)}, u32[]{:S(2)}) async-start(f32[64,1,192]{2,1,0:T(1,128)} %reshape.145), calls=%async_computation | async-start | bytes 131072 | tf_op jit(solution)/shard_map/while/body/eval_jaxpr/all_to_all | solution.py:42
  319.7 29.1 %collective-permute-start.2 = (f32[6,66,1]{2,1,0:T(8,128)S(1)}, f32[6,66,1]{2,1,0:T(8,128)S(1)}, u32[]{:S(2)}, u32[]{:S(2)}) collective-permute-start(f32[6,66,1]{2,1,0:T(8,128)S(1)} %get-tuple-element.180), channel_id=1, source_target_pairs={{0,1},{1,2},{2,3},{3,4},{4,5},{5,6},{6,7},{8,9},{9,10},{10,11},{11... | collective-permute-start | bytes 4760 | tf_op jit(solution)/shard_map/while/body/eval_jaxpr/ppermute | solution.py:16
  364.1 24.8 %all-to-all-start = ((f32[64,1,192]{2,1,0:T(1,128)}), f32[64,1,192]{2,1,0:T(1,128)S(1)}, u32[]{:S(2)}, u32[]{:S(2)}) async-start(f32[64,1,192]{2,1,0:T(1,128)} %reshape.145), calls=%async_computation | async-start | bytes 131072 | tf_op jit(solution)/shard_map/while/body/eval_jaxpr/all_to_all | solution.py:42
  382.4 29.1 %collective-permute-start.2 = (f32[6,66,1]{2,1,0:T(8,128)S(1)}, f32[6,66,1]{2,1,0:T(8,128)S(1)}, u32[]{:S(2)}, u32[]{:S(2)}) collective-permute-start(f32[6,66,1]{2,1,0:T(8,128)S(1)} %get-tuple-element.180), channel_id=1, source_target_pairs={{0,1},{1,2},{2,3},{3,4},{4,5},{5,6},{6,7},{8,9},{9,10},{10,11},{11... | collective-permute-start | bytes 4760 | tf_op jit(solution)/shard_map/while/body/eval_jaxpr/ppermute | solution.py:16
  387.0 24.5 %collective-permute-start.3 = (f32[6,66,1]{2,1,0:T(8,128)S(1)}, f32[6,66,1]{2,1,0:T(8,128)S(1)}, u32[]{:S(2)}, u32[]{:S(2)}) collective-permute-start(f32[6,66,1]{2,1,0:T(8,128)S(1)} %get-tuple-element.181), channel_id=1, source_target_pairs={{1,0},{2,1},{3,2},{4,3},{5,4},{6,5},{7,6},{9,8},{10,9},{11,10},{12... | collective-permute-start | bytes 4760 | tf_op jit(solution)/shard_map/while/body/eval_jaxpr/ppermute | solution.py:17
  426.8 24.8 %all-to-all-start = ((f32[64,1,192]{2,1,0:T(1,128)}), f32[64,1,192]{2,1,0:T(1,128)S(1)}, u32[]{:S(2)}, u32[]{:S(2)}) async-start(f32[64,1,192]{2,1,0:T(1,128)} %reshape.145), calls=%async_computation | async-start | bytes 131072 | tf_op jit(solution)/shard_map/while/body/eval_jaxpr/all_to_all | solution.py:42
  445.1 29.1 %collective-permute-start.2 = (f32[6,66,1]{2,1,0:T(8,128)S(1)}, f32[6,66,1]{2,1,0:T(8,128)S(1)}, u32[]{:S(2)}, u32[]{:S(2)}) collective-permute-start(f32[6,66,1]{2,1,0:T(8,128)S(1)} %get-tuple-element.180), channel_id=1, source_target_pairs={{0,1},{1,2},{2,3},{3,4},{4,5},{5,6},{6,7},{8,9},{9,10},{10,11},{11... | collective-permute-start | bytes 4760 | tf_op jit(solution)/shard_map/while/body/eval_jaxpr/ppermute | solution.py:16
  489.6 24.8 %all-to-all-start = ((f32[64,1,192]{2,1,0:T(1,128)}), f32[64,1,192]{2,1,0:T(1,128)S(1)}, u32[]{:S(2)}, u32[]{:S(2)}) async-start(f32[64,1,192]{2,1,0:T(1,128)} %reshape.145), calls=%async_computation | async-start | bytes 131072 | tf_op jit(solution)/shard_map/while/body/eval_jaxpr/all_to_all | solution.py:42
  507.8 29.1 %collective-permute-start.2 = (f32[6,66,1]{2,1,0:T(8,128)S(1)}, f32[6,66,1]{2,1,0:T(8,128)S(1)}, u32[]{:S(2)}, u32[]{:S(2)}) collective-permute-start(f32[6,66,1]{2,1,0:T(8,128)S(1)} %get-tuple-element.180), channel_id=1, source_target_pairs={{0,1},{1,2},{2,3},{3,4},{4,5},{5,6},{6,7},{8,9},{9,10},{10,11},{11... | collective-permute-start | bytes 4760 | tf_op jit(solution)/shard_map/while/body/eval_jaxpr/ppermute | solution.py:16
  512.4 24.5 %collective-permute-start.3 = (f32[6,66,1]{2,1,0:T(8,128)S(1)}, f32[6,66,1]{2,1,0:T(8,128)S(1)}, u32[]{:S(2)}, u32[]{:S(2)}) collective-permute-start(f32[6,66,1]{2,1,0:T(8,128)S(1)} %get-tuple-element.181), channel_id=1, source_target_pairs={{1,0},{2,1},{3,2},{4,3},{5,4},{6,5},{7,6},{9,8},{10,9},{11,10},{12... | collective-permute-start | bytes 4760 | tf_op jit(solution)/shard_map/while/body/eval_jaxpr/ppermute | solution.py:17
  552.3 24.8 %all-to-all-start = ((f32[64,1,192]{2,1,0:T(1,128)}), f32[64,1,192]{2,1,0:T(1,128)S(1)}, u32[]{:S(2)}, u32[]{:S(2)}) async-start(f32[64,1,192]{2,1,0:T(1,128)} %reshape.145), calls=%async_computation | async-start | bytes 131072 | tf_op jit(solution)/shard_map/while/body/eval_jaxpr/all_to_all | solution.py:42
  570.5 29.1 %collective-permute-start.2 = (f32[6,66,1]{2,1,0:T(8,128)S(1)}, f32[6,66,1]{2,1,0:T(8,128)S(1)}, u32[]{:S(2)}, u32[]{:S(2)}) collective-permute-start(f32[6,66,1]{2,1,0:T(8,128)S(1)} %get-tuple-element.180), channel_id=1, source_target_pairs={{0,1},{1,2},{2,3},{3,4},{4,5},{5,6},{6,7},{8,9},{9,10},{10,11},{11... | collective-permute-start | bytes 4760 | tf_op jit(solution)/shard_map/while/body/eval_jaxpr/ppermute | solution.py:16
  575.1 24.5 %collective-permute-start.3 = (f32[6,66,1]{2,1,0:T(8,128)S(1)}, f32[6,66,1]{2,1,0:T(8,128)S(1)}, u32[]{:S(2)}, u32[]{:S(2)}) collective-permute-start(f32[6,66,1]{2,1,0:T(8,128)S(1)} %get-tuple-element.181), channel_id=1, source_target_pairs={{1,0},{2,1},{3,2},{4,3},{5,4},{6,5},{7,6},{9,8},{10,9},{11,10},{12... | collective-permute-start | bytes 4760 | tf_op jit(solution)/shard_map/while/body/eval_jaxpr/ppermute | solution.py:17
  615.0 24.8 %all-to-all-start = ((f32[64,1,192]{2,1,0:T(1,128)}), f32[64,1,192]{2,1,0:T(1,128)S(1)}, u32[]{:S(2)}, u32[]{:S(2)}) async-start(f32[64,1,192]{2,1,0:T(1,128)} %reshape.145), calls=%async_computation | async-start | bytes 131072 | tf_op jit(solution)/shard_map/while/body/eval_jaxpr/all_to_all | solution.py:42
  633.2 29.1 %collective-permute-start.2 = (f32[6,66,1]{2,1,0:T(8,128)S(1)}, f32[6,66,1]{2,1,0:T(8,128)S(1)}, u32[]{:S(2)}, u32[]{:S(2)}) collective-permute-start(f32[6,66,1]{2,1,0:T(8,128)S(1)} %get-tuple-element.180), channel_id=1, source_target_pairs={{0,1},{1,2},{2,3},{3,4},{4,5},{5,6},{6,7},{8,9},{9,10},{10,11},{11... | collective-permute-start | bytes 4760 | tf_op jit(solution)/shard_map/while/body/eval_jaxpr/ppermute | solution.py:16
  677.7 24.8 %all-to-all-start = ((f32[64,1,192]{2,1,0:T(1,128)}), f32[64,1,192]{2,1,0:T(1,128)S(1)}, u32[]{:S(2)}, u32[]{:S(2)}) async-start(f32[64,1,192]{2,1,0:T(1,128)} %reshape.145), calls=%async_computation | async-start | bytes 131072 | tf_op jit(solution)/shard_map/while/body/eval_jaxpr/all_to_all | solution.py:42
  696.0 29.1 %collective-permute-start.2 = (f32[6,66,1]{2,1,0:T(8,128)S(1)}, f32[6,66,1]{2,1,0:T(8,128)S(1)}, u32[]{:S(2)}, u32[]{:S(2)}) collective-permute-start(f32[6,66,1]{2,1,0:T(8,128)S(1)} %get-tuple-element.180), channel_id=1, source_target_pairs={{0,1},{1,2},{2,3},{3,4},{4,5},{5,6},{6,7},{8,9},{9,10},{10,11},{11... | collective-permute-start | bytes 4760 | tf_op jit(solution)/shard_map/while/body/eval_jaxpr/ppermute | solution.py:16
  700.6 24.5 %collective-permute-start.3 = (f32[6,66,1]{2,1,0:T(8,128)S(1)}, f32[6,66,1]{2,1,0:T(8,128)S(1)}, u32[]{:S(2)}, u32[]{:S(2)}) collective-permute-start(f32[6,66,1]{2,1,0:T(8,128)S(1)} %get-tuple-element.181), channel_id=1, source_target_pairs={{1,0},{2,1},{3,2},{4,3},{5,4},{6,5},{7,6},{9,8},{10,9},{11,10},{12... | collective-permute-start | bytes 4760 | tf_op jit(solution)/shard_map/while/body/eval_jaxpr/ppermute | solution.py:17
  740.4 24.8 %all-to-all-start = ((f32[64,1,192]{2,1,0:T(1,128)}), f32[64,1,192]{2,1,0:T(1,128)S(1)}, u32[]{:S(2)}, u32[]{:S(2)}) async-start(f32[64,1,192]{2,1,0:T(1,128)} %reshape.145), calls=%async_computation | async-start | bytes 131072 | tf_op jit(solution)/shard_map/while/body/eval_jaxpr/all_to_all | solution.py:42
  758.7 29.1 %collective-permute-start.2 = (f32[6,66,1]{2,1,0:T(8,128)S(1)}, f32[6,66,1]{2,1,0:T(8,128)S(1)}, u32[]{:S(2)}, u32[]{:S(2)}) collective-permute-start(f32[6,66,1]{2,1,0:T(8,128)S(1)} %get-tuple-element.180), channel_id=1, source_target_pairs={{0,1},{1,2},{2,3},{3,4},{4,5},{5,6},{6,7},{8,9},{9,10},{10,11},{11... | collective-permute-start | bytes 4760 | tf_op jit(solution)/shard_map/while/body/eval_jaxpr/ppermute | solution.py:16
  803.2 24.8 %all-to-all-start = ((f32[64,1,192]{2,1,0:T(1,128)}), f32[64,1,192]{2,1,0:T(1,128)S(1)}, u32[]{:S(2)}, u32[]{:S(2)}) async-start(f32[64,1,192]{2,1,0:T(1,128)} %reshape.145), calls=%async_computation | async-start | bytes 131072 | tf_op jit(solution)/shard_map/while/body/eval_jaxpr/all_to_all | solution.py:42
  821.4 29.1 %collective-permute-start.2 = (f32[6,66,1]{2,1,0:T(8,128)S(1)}, f32[6,66,1]{2,1,0:T(8,128)S(1)}, u32[]{:S(2)}, u32[]{:S(2)}) collective-permute-start(f32[6,66,1]{2,1,0:T(8,128)S(1)} %get-tuple-element.180), channel_id=1, source_target_pairs={{0,1},{1,2},{2,3},{3,4},{4,5},{5,6},{6,7},{8,9},{9,10},{10,11},{11... | collective-permute-start | bytes 4760 | tf_op jit(solution)/shard_map/while/body/eval_jaxpr/ppermute | solution.py:16
  865.9 24.8 %all-to-all-start = ((f32[64,1,192]{2,1,0:T(1,128)}), f32[64,1,192]{2,1,0:T(1,128)S(1)}, u32[]{:S(2)}, u32[]{:S(2)}) async-start(f32[64,1,192]{2,1,0:T(1,128)} %reshape.145), calls=%async_computation | async-start | bytes 131072 | tf_op jit(solution)/shard_map/while/body/eval_jaxpr/all_to_all | solution.py:42
  884.1 29.1 %collective-permute-start.2 = (f32[6,66,1]{2,1,0:T(8,128)S(1)}, f32[6,66,1]{2,1,0:T(8,128)S(1)}, u32[]{:S(2)}, u32[]{:S(2)}) collective-permute-start(f32[6,66,1]{2,1,0:T(8,128)S(1)} %get-tuple-element.180), channel_id=1, source_target_pairs={{0,1},{1,2},{2,3},{3,4},{4,5},{5,6},{6,7},{8,9},{9,10},{10,11},{11... | collective-permute-start | bytes 4760 | tf_op jit(solution)/shard_map/while/body/eval_jaxpr/ppermute | solution.py:16
  888.7 24.5 %collective-permute-start.3 = (f32[6,66,1]{2,1,0:T(8,128)S(1)}, f32[6,66,1]{2,1,0:T(8,128)S(1)}, u32[]{:S(2)}, u32[]{:S(2)}) collective-permute-start(f32[6,66,1]{2,1,0:T(8,128)S(1)} %get-tuple-element.181), channel_id=1, source_target_pairs={{1,0},{2,1},{3,2},{4,3},{5,4},{6,5},{7,6},{9,8},{10,9},{11,10},{12... | collective-permute-start | bytes 4760 | tf_op jit(solution)/shard_map/while/body/eval_jaxpr/ppermute | solution.py:17
  928.6 24.8 %all-to-all-start = ((f32[64,1,192]{2,1,0:T(1,128)}), f32[64,1,192]{2,1,0:T(1,128)S(1)}, u32[]{:S(2)}, u32[]{:S(2)}) async-start(f32[64,1,192]{2,1,0:T(1,128)} %reshape.145), calls=%async_computation | async-start | bytes 131072 | tf_op jit(solution)/shard_map/while/body/eval_jaxpr/all_to_all | solution.py:42
  946.8 29.1 %collective-permute-start.2 = (f32[6,66,1]{2,1,0:T(8,128)S(1)}, f32[6,66,1]{2,1,0:T(8,128)S(1)}, u32[]{:S(2)}, u32[]{:S(2)}) collective-permute-start(f32[6,66,1]{2,1,0:T(8,128)S(1)} %get-tuple-element.180), channel_id=1, source_target_pairs={{0,1},{1,2},{2,3},{3,4},{4,5},{5,6},{6,7},{8,9},{9,10},{10,11},{11... | collective-permute-start | bytes 4760 | tf_op jit(solution)/shard_map/while/body/eval_jaxpr/ppermute | solution.py:16
  991.3 24.8 %all-to-all-start = ((f32[64,1,192]{2,1,0:T(1,128)}), f32[64,1,192]{2,1,0:T(1,128)S(1)}, u32[]{:S(2)}, u32[]{:S(2)}) async-start(f32[64,1,192]{2,1,0:T(1,128)} %reshape.145), calls=%async_computation | async-start | bytes 131072 | tf_op jit(solution)/shard_map/while/body/eval_jaxpr/all_to_all | solution.py:42
  1009.6 29.1 %collective-permute-start.2 = (f32[6,66,1]{2,1,0:T(8,128)S(1)}, f32[6,66,1]{2,1,0:T(8,128)S(1)}, u32[]{:S(2)}, u32[]{:S(2)}) collective-permute-start(f32[6,66,1]{2,1,0:T(8,128)S(1)} %get-tuple-element.180), channel_id=1, source_target_pairs={{0,1},{1,2},{2,3},{3,4},{4,5},{5,6},{6,7},{8,9},{9,10},{10,11},{11... | collective-permute-start | bytes 4760 | tf_op jit(solution)/shard_map/while/body/eval_jaxpr/ppermute | solution.py:16
  1054.0 24.8 %all-to-all-start = ((f32[64,1,192]{2,1,0:T(1,128)}), f32[64,1,192]{2,1,0:T(1,128)S(1)}, u32[]{:S(2)}, u32[]{:S(2)}) async-start(f32[64,1,192]{2,1,0:T(1,128)} %reshape.145), calls=%async_computation | async-start | bytes 131072 | tf_op jit(solution)/shard_map/while/body/eval_jaxpr/all_to_all | solution.py:42
  1072.3 29.1 %collective-permute-start.2 = (f32[6,66,1]{2,1,0:T(8,128)S(1)}, f32[6,66,1]{2,1,0:T(8,128)S(1)}, u32[]{:S(2)}, u32[]{:S(2)}) collective-permute-start(f32[6,66,1]{2,1,0:T(8,128)S(1)} %get-tuple-element.180), channel_id=1, source_target_pairs={{0,1},{1,2},{2,3},{3,4},{4,5},{5,6},{6,7},{8,9},{9,10},{10,11},{11... | collective-permute-start | bytes 4760 | tf_op jit(solution)/shard_map/while/body/eval_jaxpr/ppermute | solution.py:16
  1076.9 24.5 %collective-permute-start.3 = (f32[6,66,1]{2,1,0:T(8,128)S(1)}, f32[6,66,1]{2,1,0:T(8,128)S(1)}, u32[]{:S(2)}, u32[]{:S(2)}) collective-permute-start(f32[6,66,1]{2,1,0:T(8,128)S(1)} %get-tuple-element.181), channel_id=1, source_target_pairs={{1,0},{2,1},{3,2},{4,3},{5,4},{6,5},{7,6},{9,8},{10,9},{11,10},{12... | collective-permute-start | bytes 4760 | tf_op jit(solution)/shard_map/while/body/eval_jaxpr/ppermute | solution.py:17
  1116.8 24.8 %all-to-all-start = ((f32[64,1,192]{2,1,0:T(1,128)}), f32[64,1,192]{2,1,0:T(1,128)S(1)}, u32[]{:S(2)}, u32[]{:S(2)}) async-start(f32[64,1,192]{2,1,0:T(1,128)} %reshape.145), calls=%async_computation | async-start | bytes 131072 | tf_op jit(solution)/shard_map/while/body/eval_jaxpr/all_to_all | solution.py:42
  1135.0 29.1 %collective-permute-start.2 = (f32[6,66,1]{2,1,0:T(8,128)S(1)}, f32[6,66,1]{2,1,0:T(8,128)S(1)}, u32[]{:S(2)}, u32[]{:S(2)}) collective-permute-start(f32[6,66,1]{2,1,0:T(8,128)S(1)} %get-tuple-element.180), channel_id=1, source_target_pairs={{0,1},{1,2},{2,3},{3,4},{4,5},{5,6},{6,7},{8,9},{9,10},{10,11},{11... | collective-permute-start | bytes 4760 | tf_op jit(solution)/shard_map/while/body/eval_jaxpr/ppermute | solution.py:16
  1179.5 24.8 %all-to-all-start = ((f32[64,1,192]{2,1,0:T(1,128)}), f32[64,1,192]{2,1,0:T(1,128)S(1)}, u32[]{:S(2)}, u32[]{:S(2)}) async-start(f32[64,1,192]{2,1,0:T(1,128)} %reshape.145), calls=%async_computation | async-start | bytes 131072 | tf_op jit(solution)/shard_map/while/body/eval_jaxpr/all_to_all | solution.py:42
  1197.7 29.1 %collective-permute-start.2 = (f32[6,66,1]{2,1,0:T(8,128)S(1)}, f32[6,66,1]{2,1,0:T(8,128)S(1)}, u32[]{:S(2)}, u32[]{:S(2)}) collective-permute-start(f32[6,66,1]{2,1,0:T(8,128)S(1)} %get-tuple-element.180), channel_id=1, source_target_pairs={{0,1},{1,2},{2,3},{3,4},{4,5},{5,6},{6,7},{8,9},{9,10},{10,11},{11... | collective-permute-start | bytes 4760 | tf_op jit(solution)/shard_map/while/body/eval_jaxpr/ppermute | solution.py:16
  1242.2 24.8 %all-to-all-start = ((f32[64,1,192]{2,1,0:T(1,128)}), f32[64,1,192]{2,1,0:T(1,128)S(1)}, u32[]{:S(2)}, u32[]{:S(2)}) async-start(f32[64,1,192]{2,1,0:T(1,128)} %reshape.145), calls=%async_computation | async-start | bytes 131072 | tf_op jit(solution)/shard_map/while/body/eval_jaxpr/all_to_all | solution.py:42
  1260.4 29.1 %collective-permute-start.2 = (f32[6,66,1]{2,1,0:T(8,128)S(1)}, f32[6,66,1]{2,1,0:T(8,128)S(1)}, u32[]{:S(2)}, u32[]{:S(2)}) collective-permute-start(f32[6,66,1]{2,1,0:T(8,128)S(1)} %get-tuple-element.180), channel_id=1, source_target_pairs={{0,1},{1,2},{2,3},{3,4},{4,5},{5,6},{6,7},{8,9},{9,10},{10,11},{11... | collective-permute-start | bytes 4760 | tf_op jit(solution)/shard_map/while/body/eval_jaxpr/ppermute | solution.py:16
  (143 other events, 3811.4 us)
